TPU v7x, 512 devices: a whole 4x4x16 slice. The times are simulated.
512 devices in a mesh: group: 64 (over x, z_hi, y), tp: 8 (over z_lo, core).
Axes of the slice: x: 4, y: 4, z: 16 (z_hi: 4, z_lo: 4; z = z_hi * 4 + z_lo), core: 2. Of those that a mesh axis runs over, the one named last changes fastest.
Arguments:
- hidden: bfloat16 [64, 128, 2048], P('group', 'tp'), may hold values from -6 to 6
- w_query: bfloat16 [2048, 1024], P(None, 'tp'), may hold values from -0.125 to 0.125
- w_key: bfloat16 [2048, 1024], P(None, 'tp'), may hold values from -0.21875 to 0.21875
- w_value: bfloat16 [2048, 1024], P(None, 'tp'), may hold values from -0.5 to 0.5
- w_out: bfloat16 [1024, 2048], P('tp'), may hold values from -0.1875 to 0.1875
- cache_keys: bfloat16 [256, 256, 1024], P(None, 'group', 'tp'), may hold values from -600 to 600
- cache_values: bfloat16 [256, 256, 1024], P(None, 'group', 'tp'), may hold values from -24 to 24
- stretch_count: int32 [64], P('group'), may hold values from 4 to 12, as said below
- stretch_ids: int32 [64, 12], P('group'), may hold values from 0 to 255
- recompute_pos: int32 [64, 128], P('group'), may hold values from 0 to 3071, as said below
Outputs:
- merged_out: bfloat16 [64, 128, 2048], P('group', 'tp')
Inputs may be any that keep to these rules, and one draw needn't show every extreme that they name: `stretch_count`: some request joins exactly 12 stretches and some exactly 4. `stretch_ids`: entries from slot stretch_count of a request on are not used. `recompute_pos`: strictly increasing in each request; the first is 0 and the last is stretch_count * 256 - 1 of that request.
All inputs are finite; a program needn't handle non-finite values.
Results may differ from a plain program's by a relative error of at most 0.013.
The roundings to bfloat16 on the way count: a program that leaves them out, or rounds other values in their place, can miss the bound.
Values may be sent and summed in bfloat16 or wider, within the bound.
A program may use at most 64 MiB of HBM per device.

v0:
```python
import jax
import jax.numpy as jnp
from jax import lax
from jax.sharding import PartitionSpec as P

HEAD_DIM = 64
STRETCH = 256
MAXCH = 12


ROPE_BASE = 130000.0
EPSILON = 1e-05


def rope_tables(positions, head_dim):
    half_dim = head_dim // 2
    frequency = ROPE_BASE ** (-(jnp.arange(half_dim, dtype=jnp.float32) * 2.0 / head_dim))
    angles = positions.astype(jnp.float32)[..., None] * frequency
    return (jnp.cos(angles), jnp.sin(angles))


def rotate_half(values, cosine_table, sine_table):
    half_dim = values.shape[-1] // 2
    lower_half = values[..., :half_dim]
    upper_half = values[..., half_dim:]
    return jnp.concatenate(
        [
            lower_half * cosine_table - upper_half * sine_table,
            upper_half * cosine_table + lower_half * sine_table,
        ],
        axis=-1,
    )


def mark_rows(positions, slot_count, stretch_len):
    marks = jnp.zeros((slot_count * stretch_len,), jnp.int32).at[positions].set(1)
    return marks.reshape(slot_count, stretch_len)


def weigh(scores, usable, row_max):
    weights = jnp.where(usable, jnp.exp(scores - row_max[..., None]), 0.0)
    return (jnp.sum(weights, axis=-1), weights.astype(jnp.bfloat16))


def local(
    hidden,
    w_query,
    w_key,
    w_value,
    w_out,
    cache_keys,
    cache_values,
    stretch_count,
    stretch_ids,
    recompute_pos,
):
    head_dim = HEAD_DIM
    stretch_len = STRETCH
    slot_count = MAXCH
    local_width = w_query.shape[1]
    local_heads = local_width // head_dim
    row_count = recompute_pos.shape[1]
    group_count = lax.axis_size("group")
    my_group = lax.axis_index("group")
    score_scale = head_dim ** (-0.5)
    full_rows = lax.all_gather(hidden, "tp", axis=1, tiled=True)[0].astype(jnp.float32)
    normed = (
        full_rows * lax.rsqrt(jnp.mean(full_rows * full_rows, axis=-1, keepdims=True) + EPSILON)
    ).astype(jnp.bfloat16)
    own_positions = recompute_pos[0]
    query_cos, query_sin = rope_tables(own_positions, head_dim)

    def project(weight):
        return jnp.dot(normed, weight, preferred_element_type=jnp.float32).reshape(
            row_count, local_heads, head_dim
        )

    own_queries = rotate_half(
        project(w_query), query_cos[:, None, :], query_sin[:, None, :]
    ).astype(jnp.bfloat16)
    fresh_keys = rotate_half(project(w_key), query_cos[:, None, :], query_sin[:, None, :]).astype(
        jnp.bfloat16
    )
    fresh_values = project(w_value).astype(jnp.bfloat16)
    counts_all, stretches_all = (
        lax.all_gather(stretch_count, "group", axis=0, tiled=True),
        lax.all_gather(stretch_ids, "group", axis=0, tiled=True),
    )
    destination = jnp.arange(group_count, dtype=jnp.int32)
    slot_range = jnp.arange(slot_count, dtype=jnp.int32)
    owner_req = jnp.broadcast_to(destination[:, None], (group_count, slot_count))
    slot_place = jnp.broadcast_to(slot_range[None, :], (group_count, slot_count))
    slot_place = jnp.clip(slot_place, 0, slot_count - 1)
    wanted = jnp.transpose(stretches_all[owner_req, slot_place])
    send_keys = cache_keys[wanted]
    send_values = cache_values[wanted]
    got_keys, got_values = (
        lax.all_to_all(send_keys, "group", split_axis=1, concat_axis=1, tiled=True),
        lax.all_to_all(send_values, "group", split_axis=1, concat_axis=1, tiled=True),
    )
    my_place = slot_place[my_group]
    own_slots = owner_req[my_group] == my_group
    my_live = counts_all[my_group]
    offset_cos, offset_sin = rope_tables(my_place * stretch_len, head_dim)
    key_buffer = rotate_half(
        got_keys.reshape(slot_count, stretch_len, local_heads, head_dim).astype(jnp.float32),
        offset_cos[:, None, None, :],
        offset_sin[:, None, None, :],
    ).astype(jnp.bfloat16)
    value_buffer = got_values.reshape(slot_count, stretch_len, local_heads, head_dim)
    own_marks = mark_rows(own_positions, slot_count, stretch_len)

    def masked_scores(slot_index):
        own_slot = own_slots[slot_index]
        place_now = my_place[slot_index]
        queries = jnp.where(own_slot, own_queries, own_queries)
        positions = jnp.where(own_slot, own_positions, own_positions)
        skipped = jnp.where(own_slot, own_marks[place_now], own_marks[place_now])
        key_positions = place_now * stretch_len + jnp.arange(stretch_len, dtype=jnp.int32)
        usable = (skipped == 0)[None, :] & (key_positions[None, :] <= positions[:, None])
        scores = (
            jnp.einsum(
                "qhd,khd->hqk", queries, key_buffer[slot_index], preferred_element_type=jnp.float32
            )
            * score_scale
        )
        return jnp.where(usable[None], scores, -jnp.inf)

    def max_step(slot_index, carry):
        own_max, their_max, score_store = carry
        own_slot = own_slots[slot_index]
        scores = masked_scores(slot_index)
        slot_max = jnp.max(scores, axis=-1)
        score_store = lax.dynamic_update_index_in_dim(score_store, scores, slot_index, 0)
        return (
            jnp.where(own_slot, jnp.maximum(own_max, slot_max), own_max),
            jnp.where(own_slot, their_max, jnp.maximum(their_max, slot_max)),
            score_store,
        )

    fresh_scores = (
        jnp.einsum("qhd,khd->hqk", own_queries, fresh_keys, preferred_element_type=jnp.float32)
        * score_scale
    )
    fresh_usable = own_positions[None, :] <= own_positions[:, None]
    start_max = jnp.max(jnp.where(fresh_usable[None], fresh_scores, -jnp.inf), axis=-1)
    lowest = jnp.full((local_heads, row_count), -jnp.inf, jnp.float32)
    empty_store = jnp.full((slot_count, local_heads, row_count, stretch_len), -jnp.inf, jnp.float32)
    own_max, their_max, score_store = lax.fori_loop(
        0, my_live, max_step, (start_max, lowest, empty_store)
    )
    own_final = own_max
    their_final = their_max

    def sum_step(slot_index, carry):
        own_out, own_den, their_out, their_den = carry
        own_slot = own_slots[slot_index]
        scores = score_store[slot_index]
        row_max = jnp.where(own_slot, own_final, their_final)
        slot_den, slot_weights = weigh(scores, scores > -jnp.inf, row_max)
        slot_out = jnp.einsum(
            "hqk,khd->qhd",
            slot_weights,
            value_buffer[slot_index],
            preferred_element_type=jnp.float32,
        )
        return (
            jnp.where(own_slot, own_out + slot_out, own_out),
            jnp.where(own_slot, own_den + slot_den, own_den),
            jnp.where(own_slot, their_out, their_out + slot_out),
            jnp.where(own_slot, their_den, their_den + slot_den),
        )

    fresh_den, fresh_weights = weigh(fresh_scores, fresh_usable[None], own_final)
    fresh_out = jnp.einsum(
        "hqk,khd->qhd", fresh_weights, fresh_values, preferred_element_type=jnp.float32
    )
    empty_out = jnp.zeros((row_count, local_heads, head_dim), jnp.float32)
    empty_den = jnp.zeros((local_heads, row_count), jnp.float32)
    own_out, own_den, their_out, their_den = lax.fori_loop(
        0, my_live, sum_step, (fresh_out, fresh_den, empty_out, empty_den)
    )
    attention = (
        (own_out / jnp.transpose(own_den)[:, :, None])
        .astype(jnp.bfloat16)
        .reshape(row_count, local_width)
    )
    mixed = lax.psum_scatter(
        jnp.dot(attention, w_out, preferred_element_type=jnp.float32),
        "tp",
        scatter_dimension=0,
        tiled=True,
    )
    return mixed.astype(jnp.bfloat16)[None]


def solution(mesh):
    placed = (
        P("group", "tp", None),
        P(None, "tp"),
        P(None, "tp"),
        P(None, "tp"),
        P("tp", None),
        P(None, "group", "tp"),
        P(None, "group", "tp"),
        P("group"),
        P("group", None),
        P("group", None),
    )
    return jax.shard_map(
        local, mesh=mesh, in_specs=placed, out_specs=P("group", "tp", None), check_vma=False
    )
```

profile of v0, /device:TPU:1, one launch (start us, length us, event | category | flops | bytes accessed | tf_op | source)
XLA Modules:
  0.0 537.2 jit_solution(6657135579154290848)
XLA Ops:
  6.7 200.1 %all-gather = s32[64,1,12]{2,1,0:T(1,128)S(1)} all-gather(s32[1,1,12]{2,1,0:T(1,128)} %bitcast.111), channel_id=1, replica_groups=mesh['group'=64,'tp'=8] {'group'}, dimensions={0}, use_global_device_ids=true | all-gather | bytes 3120 | tf_op jit(solution)/shard_map/all_gather | solution.py:87
  206.7 5.1 gather_fusion
  212.2 2.8 gather_fusion.1
  215.0 1.2 copy.67
  216.2 4.6 all-to-all-start
  222.8 1.3 dynamic-slice.2
  224.8 30.7 %all-reduce = s32[64]{0:T(128)S(1)} all-reduce(s32[64]{0:T(128)S(1)} %dynamic-update-slice), channel_id=1, replica_groups=mesh['group'=64,'tp'=8] {'group'}, use_global_device_ids=true, to_apply=%add | all-reduce | flops 64 | bytes 512
  257.2 2.1 copy.62
  259.3 2.8 gather_fusion.2
  262.2 1.1 copy.73
  263.9 50.1 %all_gather.9 = bf16[1,128,2048]{2,1,0:T(8,128)(2,1)S(1)} all-gather(bf16[1,16,2048]{2,1,0:T(8,128)(2,1)S(1)} %copy-done.7), channel_id=1, replica_groups=mesh['group'=64,'tp'=8] {'tp'}, dimensions={1}, use_global_device_ids=true | all-gather | bytes 589824 | tf_op jit(solution)/shard_map/all_gather | solution.py:66
  314.4 1.4 fusion.37
  317.3 8.5 %all-to-all-start.1 = ((bf16[12,64,4,128]{3,2,0,1:T(4,128)(2,1)}), bf16[12,64,4,128]{3,2,0,1:T(4,128)(2,1)S(1)}, u32[]{:S(2)}, u32[]{:S(2)}) async-start(bf16[12,64,4,128]{3,2,0,1:T(4,128)(2,1)} %copy.73), calls=%async_computation.1 | async-start | bytes 1572864 | tf_op jit(solution)/shard_map/all_to_all | solution.py:99
  327.3 3.2 reshape.297
  330.6 6.5 %subtract_convert_fusion = (bf16[12,256,2,32]{3,2,1,0:T(2,128)(2,1)S(1)}, bf16[12,256,2,32]{3,2,1,0:T(2,128)(2,1)S(1)}) fusion(f32[12,256,2,64]{3,2,1,0:T(2,128)} %reshape.297, f32[12,32]{1,0:T(8,128)S(1)} %get-tuple-element.309, f32[12,32]{1,0:T(8,128)S(1)} %get-tuple-element.308), kind=kLoop, calls=%fused_computation.37 | loop fusion | flops 1572864 | bytes 2362368 | tf_op jit(solution)/shard_map/convert.1
  337.1 4.3 pad_maximum_fusion
  341.5 2.6 copy.70
  344.0 2.0 broadcast_in_dim.64
  346.1 64.1 %while.29 = (s32[]{:T(128)}, f32[2,128]{1,0:T(2,128)S(1)}, f32[2,128]{1,0:T(2,128)S(1)}, f32[12,2,128,256]{2,3,1,0:T(8,128)}, s32[]{:T(128)}, /*index=5*/pred[12...) while((s32[]{:T(128)}, f32[2,128]{1,0:T(2,128)S(1)}, ...), condition=%wide.region_5.6_spmd, body=%wide.region_3.5_spmd.sunk | while | flops 8652041 | bytes 960768 | solution.py:149
  350.1 1.1 fusion.58
  357.1 1.1 fusion.58
  364.2 1.1 fusion.58
  371.2 1.1 fusion.58
  378.3 1.1 fusion.58
  385.3 1.1 fusion.58
  392.4 1.1 fusion.58
  399.4 1.1 fusion.58
  406.5 1.1 fusion.58
  412.8 40.7 %while.30 = (s32[]{:T(128)}, f32[128,2,64]{0,2,1:T(8,128)S(1)}, f32[2,128]{1,0:T(2,128)S(1)}, s32[]{:T(128)}, pred[12]{0:T(512)(128)(4,1)S(1)}, /*index=5*/bf16[...) while((s32[]{:T(128)}, f32[128,2,64]{0,2,1:T(8,128)S(1)}, ...), condition=%wide.region_9.10_spmd, body=%wide.region_7.9_spmd.sunk | while | flops 8946181 | bytes 1778856 | solution.py:180
  453.5 1.3 fusion.44
  454.8 73.9 %reduce-scatter.2.cloned.1.call-done = f32[16,2048]{1,0:T(8,128)} async-done(((f32[128,2048]{1,0:T(8,128)}), f32[16,2048]{1,0:T(8,128)}) %reduce-scatter.2.cloned.1.call-update) | async-done | bytes 131088 | tf_op jit(solution)/shard_map/reduce_scatter | solution.py:188
  528.8 1.5 convert_bitcast_fusion
  (196 shorter events, 69.0 us)
Async XLA Ops:
  6.5 447.0 %copy-start = (bf16[128,2048]{1,0:T(8,128)(2,1)S(1)}, bf16[128,2048]{1,0:T(8,128)(2,1)}, u32[]{:S(2)}) copy-start(bf16[128,2048]{1,0:T(8,128)(2,1)} %param.18) | copy-start | bytes 1572868
  206.7 5.5 %copy-start.1 = (bf16[256,4,128]{2,1,0:T(4,128)(2,1)S(1)}, bf16[256,4,128]{2,1,0:T(4,128)(2,1)}, u32[]{:S(2)}) copy-start(bf16[256,4,128]{2,1,0:T(4,128)(2,1)} %param.19) | copy-start | bytes 786436
  211.9 9.0 %copy-start.3 = (bf16[2048,128]{1,0:T(8,128)(2,1)S(1)}, bf16[2048,128]{1,0:T(8,128)(2,1)}, u32[]{:S(2)}) copy-start(bf16[2048,128]{1,0:T(8,128)(2,1)} %param.16) | copy-start | bytes 1572868
  211.9 10.0 %copy-start.4 = (bf16[2048,128]{1,0:T(8,128)(2,1)S(1)}, bf16[2048,128]{1,0:T(8,128)(2,1)}, u32[]{:S(2)}) copy-start(bf16[2048,128]{1,0:T(8,128)(2,1)} %param.15) | copy-start | bytes 1572868
  212.2 44.0 %copy-start.8 = (s32[1,128]{1,0:T(1,128)S(1)}, s32[1,128]{1,0:T(1,128)}, u32[]{:S(2)}) copy-start(s32[1,128]{1,0:T(1,128)} %param.23) | copy-start | bytes 1540
  215.0 44.3 %copy-start.2 = (bf16[256,4,128]{2,1,0:T(4,128)(2,1)S(1)}, bf16[256,4,128]{2,1,0:T(4,128)(2,1)}, u32[]{:S(2)}) copy-start(bf16[256,4,128]{2,1,0:T(4,128)(2,1)} %param.20) | copy-start | bytes 786436
  216.2 101.1 %all-to-all-start = ((bf16[12,64,4,128]{3,2,0,1:T(4,128)(2,1)}), bf16[12,64,4,128]{3,2,0,1:T(4,128)(2,1)S(1)}, u32[]{:S(2)}, u32[]{:S(2)}) async-start(bf16[12,64,4,128]{3,2,0,1:T(4,128)(2,1)} %copy.67), calls=%async_computation | async-start | bytes 1572864 | tf_op jit(solution)/shard_map/all_to_all | solution.py:98
  220.9 43.0 %copy-start.7 = (bf16[1,16,2048]{2,1,0:T(8,128)(2,1)S(1)}, bf16[1,16,2048]{2,1,0:T(8,128)(2,1)}, u32[]{:S(2)}) copy-start(bf16[1,16,2048]{2,1,0:T(8,128)(2,1)} %param.14) | copy-start | bytes 196612
  222.1 92.1 %copy-start.9 = (s32[1,128]{1,0:T(1,128)S(1)}, s32[1,128]{1,0:T(1,128)}, u32[]{:S(2)}) copy-start(s32[1,128]{1,0:T(1,128)} %param.23) | copy-start | bytes 1540
  262.2 54.1 %copy-start.10 = (s32[1,128]{1,0:T(1,128)S(1)}, s32[1,128]{1,0:T(1,128)}, u32[]{:S(2)}) copy-start(s32[1,128]{1,0:T(1,128)} %param.23) | copy-start | bytes 1540
  317.3 93.5 %all-to-all-start.1 = ((bf16[12,64,4,128]{3,2,0,1:T(4,128)(2,1)}), bf16[12,64,4,128]{3,2,0,1:T(4,128)(2,1)S(1)}, u32[]{:S(2)}, u32[]{:S(2)}) async-start(bf16[12,64,4,128]{3,2,0,1:T(4,128)(2,1)} %copy.73), calls=%async_computation.1 | async-start | bytes 1572864 | tf_op jit(solution)/shard_map/all_to_all | solution.py:99
  325.9 202.9 %reduce-scatter.2.cloned.1.call-start = ((), (), s32[]{:S(2)}) async-start(), calls=%async_computation.3 | async-start | bytes 1179648 | tf_op jit(solution)/shard_map/reduce_scatter | solution.py:188
  341.4 4.6 copy-start.11
  341.5 4.6 copy-start.12
  346.0 64.2 %copy-start.6 = (f32[2,128,128]{1,2,0:T(8,128)S(1)}, f32[2,128,128]{1,2,0:T(8,128)}, u32[]{:S(2)}) copy-start(f32[2,128,128]{1,2,0:T(8,128)} %get-tuple-element.313) | copy-start | bytes 393220
  346.0 64.2 %copy-start.5 = (bf16[2048,128]{0,1:T(8,128)(2,1)S(1)}, bf16[2048,128]{0,1:T(8,128)(2,1)}, u32[]{:S(2)}) copy-start(bf16[2048,128]{0,1:T(8,128)(2,1)} %copy.62) | copy-start | bytes 1572868
Sparse Core Ops, SparseCore 0:
  454.9 73.7 reduce-scatter.1
where the time goes:
time: 541 us; the launch traced here: 537 us
  blocking collectives  281 us (52%)
  waiting for transfers between devices  74 us (14%)
  local copies, waits for them, and re-layouts  63.8 us (12%)
  loops' own time  36.4 us (7%)
  other arithmetic  32.8 us (6%)
  matrix products  21.4 us (4%)
  between operations  14.4 us (3%)
  starting transfers between devices  13.4 us (2%)
    all_gather x1, blocking collectives, local(): lax.all_gather(stretch_ids, 'group', axis=0, tiled=True)  200 us
    reduce_scatter x1, waiting for transfers between devices, local(): lax.psum_scatter(jnp.dot(attention, w_out, preferred_element_type=jnp.flo...  73.9 us
    all_gather x1, blocking collectives, local(): lax.all_gather(hidden, 'tp', axis=1, tiled=True)[0].astype(jnp.float32)  50.1 us
    unnamed x1, blocking collectives  30.7 us
    another operation x1, loops' own time, local(): lax.fori_loop(0, my_live, max_step, (start_max, lowest, empty_store))  29.6 us
  transfers between devices with their start and end apart: 3, of which 1 were waited for; matrix products, arithmetic and copies ran while one was open for 13% of the time, Pallas kernels for 0%

commit v1 on v0

v1 whole, which is shorter than its diff:
```python
import functools

import jax
import jax.numpy as jnp
import numpy as np
from jax import lax
from jax.experimental import pallas as pl
from jax.experimental.pallas import tpu as pltpu
from jax.sharding import PartitionSpec as P

MESH = pl.DeviceIdType.MESH
HEAD_DIM = 64
STRETCH = 256
MAXCH = 12
ROPE_BASE = 130000.0
EPSILON = 1e-05
MASKED = -1e30
FLOOR = -1e29
FAR = 1 << 20


def kernel(
    hidden,
    ids,
    count,
    pos,
    freq,
    cache_keys,
    cache_values,
    w_query,
    w_key,
    w_value,
    w_out,
    out,
    normed,
    wqkv,
    wo,
    cache32,
    ids_v,
    ids_s,
    posz,
    kv_send,
    kv,
    qx,
    fresh,
    key_cos,
    key_sin,
    key_pos,
    o_send,
    o_recv,
    st_send,
    st_recv,
    att,
    att_recv,
    part,
    part_send,
    part_recv,
    sem_load,
    sem_idz_s,
    sem_idz_r,
    sem_idp_s,
    sem_idp_r,
    sem_smem,
    sem_hid_s,
    sem_hid_r,
    sem_hidp_s,
    sem_hidp_r,
    sem_kv_s,
    sem_kv_r,
    sem_q_s,
    sem_q_r,
    sem_pos_s,
    sem_pos_r,
    sem_o_s,
    sem_o_r,
    sem_st_s,
    sem_st_r,
    sem_wo_s,
    sem_wo_r,
    sem_att_s,
    sem_att_r,
    sem_part_s,
    sem_part_r,
):
    f32, bf16 = jnp.float32, jnp.bfloat16
    g, t = lax.axis_index("group"), lax.axis_index("tp")
    gx, gz, gy = g // 16, (g // 4) % 4, g % 4
    s = gx * 4 + gy
    zl, core = t // 2, t % 2
    other = 1 - core

    def plane_id(idx):
        return (((idx // 4) * 4 + gz) * 4 + idx % 4, t)

    def z_id(step):
        return ((gx * 4 + (gz + step) % 4) * 4 + gy, t)

    def run_id(step):
        return (g, ((zl + step) % 4) * 2 + core)

    partner_id = (g, zl * 2 + other)

    def remote(src, dst, send, recv, device):
        return pltpu.make_async_remote_copy(
            src_ref=src, dst_ref=dst, send_sem=send, recv_sem=recv, device_id=device, device_id_type=MESH
        )

    loads = [
        pltpu.make_async_copy(w_query, wqkv.at[:, 0:128], sem_load.at[0]),
        pltpu.make_async_copy(w_key, wqkv.at[:, 128:256], sem_load.at[1]),
        pltpu.make_async_copy(w_value, wqkv.at[:, 256:384], sem_load.at[2]),
        pltpu.make_async_copy(w_out, wo.at[0], sem_load.at[3]),
    ]
    for load in loads:
        load.start()

    barrier = pltpu.get_barrier_semaphore()

    def greet(device):
        pl.semaphore_signal(barrier, inc=1, device_id=device, device_id_type=MESH)

    for step in (2, 1, 3):
        greet(z_id(step))

    def greet_plane(d, carry):
        greet(plane_id((s + d) % 16))
        return carry

    lax.fori_loop(1, 16, greet_plane, 0)
    for step in (1, 2, 3):
        greet(run_id(step))
    greet(partner_id)

    lane = lax.broadcasted_iota(jnp.int32, (1, 128), 1)
    ids_v[s] = jnp.where(lane == MAXCH, count[0], 0)
    ids_v[s, :, 0:MAXCH] = ids[...]
    posz[0] = pos[...]
    rows = hidden[0].astype(f32)
    normed[t] = (rows * lax.rsqrt(jnp.mean(rows * rows, axis=-1, keepdims=True) + EPSILON)).astype(bf16)

    def widen(i, carry):
        here = pl.ds(pl.multiple_of(i * 32, 32), 32)
        cache32[here, 0:4, :] = cache_keys[here].astype(f32)
        cache32[here, 4:8, :] = cache_values[here].astype(f32)
        return carry

    lax.fori_loop(0, 8, widen, 0)

    row48 = lax.broadcasted_iota(jnp.int32, (48, 128), 0)
    slot_angle = ((row48 // 4) * STRETCH).astype(f32) * freq[...]
    key_cos[...] = jnp.cos(slot_angle)
    key_sin[...] = jnp.sin(slot_angle)
    row48 = lax.broadcasted_iota(jnp.int32, (16, 48, 128), 1)
    place = lax.broadcasted_iota(jnp.int32, (16, 48, 128), 0)
    key_pos[...] = (row48 // 4) * STRETCH + 4 * (16 * (place // 4) + 4 * gz + place % 4) + row48 % 4

    pl.semaphore_wait(barrier, 22)

    def id_z(step):
        return remote(ids_v.at[s], ids_v.at[(4 - step) * 16 + s], sem_idz_s.at[step], sem_idz_r.at[4 - step], z_id(step))

    def id_z_wait(dz):
        here = ids_v.at[dz * 16 + s]
        remote(here, here, sem_idz_s.at[dz], sem_idz_r.at[dz], z_id(1)).wait_recv()

    def pos_z(step):
        return remote(posz.at[0], posz.at[4 - step], sem_pos_s.at[step], sem_pos_r.at[4 - step], z_id(step))

    def id_plane(dz, d):
        here = ids_v.at[dz * 16 + s]
        return remote(here, here, sem_idp_s.at[dz, d], sem_idp_r.at[dz, d], plane_id((s + d) % 16))

    def id_plane_wait(dz, d):
        here = ids_v.at[dz * 16 + (s + 16 - d) % 16]
        return remote(here, here, sem_idp_s.at[dz, d], sem_idp_r.at[dz, d], plane_id((s + d) % 16))

    def spread_ids(dz):
        def body(d, carry):
            id_plane(dz, d).start()
            return carry

        lax.fori_loop(1, 16, body, 0)

    for step in (2, 1, 3):
        id_z(step).start()
    spread_ids(0)
    for step in (2, 1, 3):
        pos_z(step).start()

    def hid_run(step):
        here = normed.at[t]
        return remote(here, here, sem_hid_s.at[step], sem_hid_r.at[step], run_id(step))

    def hid_run_wait(step):
        here = normed.at[((zl + 4 - step) % 4) * 2 + core]
        remote(here, here, sem_hid_s.at[step], sem_hid_r.at[step], run_id(step)).wait_recv()

    def hid_pair(step):
        here = normed.at[((zl + 4 - step) % 4) * 2 + core]
        return remote(here, here, sem_hidp_s.at[step], sem_hidp_r.at[step], partner_id)

    def hid_pair_wait(step):
        here = normed.at[((zl + 4 - step) % 4) * 2 + other]
        remote(here, here, sem_hidp_s.at[step], sem_hidp_r.at[step], partner_id).wait_recv()

    for step in (1, 2, 3):
        hid_run(step).start()
    hid_pair(0).start()
    loads[3].wait()
    wo_pair = remote(wo.at[0], wo.at[1], sem_wo_s, sem_wo_r, partner_id)
    wo_pair.start()

    low_rows = lax.broadcasted_iota(jnp.int32, (8, 128), 0) < 4

    def fill(row, target):
        for quad in range(3):
            key_rows, value_rows = [], []
            for pair in range(2):
                first = cache32[ids_s[row, 0, quad * 4 + pair * 2]]
                second = cache32[ids_s[row, 0, quad * 4 + pair * 2 + 1]]
                key_rows.append(jnp.where(low_rows, first, pltpu.roll(second, 4, 0)))
                value_rows.append(jnp.where(low_rows, pltpu.roll(first, 4, 0), second))
            target[quad * 16 : quad * 16 + 16, :] = jnp.concatenate(key_rows, 0).astype(bf16)
            target[48 + quad * 16 : 64 + quad * 16, :] = jnp.concatenate(value_rows, 0).astype(bf16)

    def kv_copy(dz, d):
        return remote(
            kv_send.at[dz, d], kv.at[dz, s], sem_kv_s.at[dz, d], sem_kv_r.at[dz, d], plane_id((s + d) % 16)
        )

    def serve(dz):
        def got(d, carry):
            id_plane_wait(dz, d).wait_recv()
            return carry

        lax.fori_loop(1, 16, got, 0)
        here = pl.ds(dz * 16, 16)
        to_smem = pltpu.make_async_copy(ids_v.at[here], ids_s.at[here], sem_smem.at[dz])
        to_smem.start()
        to_smem.wait()

        def send(d, carry):
            fill(dz * 16 + (s + d) % 16, kv_send.at[dz, d])
            kv_copy(dz, d).start()
            return carry

        lax.fori_loop(1, 16, send, 0)
        fill(dz * 16 + s, kv.at[dz, s])

    id_z_wait(1)
    spread_ids(1)
    id_z_wait(3)
    spread_ids(3)
    serve(0)
    id_z_wait(2)
    spread_ids(2)
    serve(1)
    serve(3)

    for step in (1, 2, 3):
        hid_run_wait(step)
        hid_pair(step).start()
    posf = jnp.broadcast_to(pos[...].astype(f32), (128, 128)).T
    angle = posf * freq[...]
    cos_q, sin_q = jnp.cos(angle), jnp.sin(angle)
    lanes = lax.broadcasted_iota(jnp.int32, (128, 128), 1)
    lower = lanes % 64 < 32
    for load in loads[:3]:
        load.wait()
    for step in range(4):
        hid_pair_wait(step)
    projected = jnp.dot(normed[...].reshape(128, 2048), wqkv[...], preferred_element_type=f32)

    def rotate(values):
        swapped = jnp.where(lower, -pltpu.roll(values, 96, 1), pltpu.roll(values, 32, 1))
        return (values * cos_q + swapped * sin_q).astype(bf16)

    qx[0] = (rotate(projected[:, 0:128]).astype(f32) * HEAD_DIM**-0.5).astype(bf16)
    fresh[0] = rotate(projected[:, 128:256])
    fresh[1] = projected[:, 256:384].astype(bf16)

    def q_z(step):
        return remote(qx.at[0], qx.at[4 - step], sem_q_s.at[step], sem_q_r.at[4 - step], z_id(step))

    for step in (2, 1, 3):
        q_z(step).start()
    serve(2)

    head0 = lanes < 64
    swap_row = lax.broadcasted_iota(jnp.int32, (128, 128), 0)
    swap = jnp.where(
        (lanes % 64 < 32) & (swap_row == lanes + 32),
        -1.0,
        jnp.where((lanes % 64 >= 32) & (swap_row == lanes - 32), 1.0, 0.0),
    ).astype(bf16)
    ones = jnp.ones((128, 128), bf16)
    last_dims = (((1,), (1,)), ((), ()))
    first_dims = (((0,), (0,)), ((), ()))

    def soften(keys, values, queries, usable):
        zero = jnp.zeros((), bf16)
        both = jnp.concatenate([jnp.where(head0, queries, zero), jnp.where(head0, zero, queries)], 0)
        scores = lax.dot_general(keys, both, last_dims, preferred_element_type=f32)
        tops, sums, weights = [], [], []
        for head in range(2):
            part_scores = jnp.where(usable, scores[:, head * 128 : head * 128 + 128], MASKED)
            top = jnp.maximum(jnp.max(part_scores, axis=0, keepdims=True), FLOOR)
            weight = jnp.exp(part_scores - top)
            tops.append(top)
            sums.append(jnp.sum(weight, axis=0, keepdims=True))
            weights.append(weight.astype(bf16))
        mixed = lax.dot_general(values, jnp.concatenate(weights, 1), first_dims, preferred_element_type=f32)
        return jnp.concatenate([mixed[0:64, 0:128], mixed[64:128, 128:256]], 0), tops, sums

    def attend(dz):
        def got(d, carry):
            here = kv.at[dz, (s + 16 - d) % 16]
            remote(here, here, sem_kv_s.at[dz, d], sem_kv_r.at[dz, d], plane_id((s + d) % 16)).wait_recv()
            return carry

        lax.fori_loop(1, 16, got, 0)
        raw = kv[dz, :, 0:48, :]
        turned = jnp.dot(raw.reshape(768, 128), swap, preferred_element_type=f32).reshape(16, 48, 128)
        keys = (raw.astype(f32) * key_cos[...][None] + turned * key_sin[...][None]).astype(bf16).reshape(768, 128)
        values = kv[dz, :, 48:96, :].reshape(768, 128)
        place_of = key_pos[...].reshape(768, 128)
        pos_row = posz[dz]
        pos_col = jnp.broadcast_to(pos_row, (768, 128))
        same = jnp.where(place_of == pos_col, 1.0, 0.0).astype(bf16)
        marked = jnp.dot(same, ones, preferred_element_type=f32) > 0.5
        limit = ids_s[dz * 16 + s, 0, MAXCH] * STRETCH
        usable = jnp.where(marked | (place_of >= limit), FAR, place_of) <= pos_col
        return soften(keys, values, qx[dz], usable)

    def o_copy(dz):
        return remote(o_send.at[dz], o_recv.at[4 - dz], sem_o_s.at[dz], sem_o_r.at[4 - dz], z_id(dz))

    def st_copy(dz):
        return remote(st_send.at[dz], st_recv.at[4 - dz], sem_st_s.at[dz], sem_st_r.at[4 - dz], z_id(dz))

    def wait_z(ref, send, recv, dz):
        here = ref.at[dz]
        remote(here, here, send.at[dz], recv.at[dz], z_id(1)).wait_recv()

    partials = [
        soften(fresh[0], fresh[1], qx[0], posf <= pos[...].astype(f32)),
        attend(0),
    ]
    for dz in (1, 3, 2):
        wait_z(posz, sem_pos_s, sem_pos_r, dz)
        wait_z(qx, sem_q_s, sem_q_r, dz)
        mixed, tops, sums = attend(dz)
        o_send[dz] = mixed.astype(bf16)
        st_send[dz] = jnp.concatenate(tops + sums, 0)
        o_copy(dz).start()
        st_copy(dz).start()
    for dz in (1, 3, 2):
        wait_z(o_recv, sem_o_s, sem_o_r, dz)
        wait_z(st_recv, sem_st_s, sem_st_r, dz)
        stats = st_recv[dz]
        partials.append(
            (o_recv[dz].astype(f32), [stats[0:1], stats[1:2]], [stats[2:3], stats[3:4]])
        )
    halves = []
    for head in range(2):
        top = functools.reduce(jnp.maximum, [tops[head] for _, tops, _ in partials])
        total, weight = 0.0, 0.0
        for mixed, tops, sums in partials:
            factor = jnp.exp(tops[head] - top)
            total = total + mixed[head * 64 : head * 64 + 64] * factor
            weight = weight + sums[head] * factor
        halves.append(total / weight)
    attention = jnp.concatenate(halves, 0).T.astype(bf16)
    for run in range(4):
        for half in range(2):
            att[half, run] = attention[run * 32 + half * 16 : run * 32 + half * 16 + 16]

    att_pair = remote(att.at[other], att_recv, sem_att_s, sem_att_r, partner_id)
    att_pair.start()
    wo_pair.wait_recv()
    att_pair.wait_recv()
    mine = jnp.concatenate([att[core].reshape(64, 128), att_recv[...].reshape(64, 128)], 1)
    product = jnp.dot(mine, wo[...].reshape(256, 2048), preferred_element_type=f32).reshape(4, 16, 2048)
    part[...] = product
    part_send[...] = product.astype(bf16)

    def part_copy(step):
        return remote(
            part_send.at[(zl + step) % 4], part_recv.at[step], sem_part_s.at[step], sem_part_r.at[step], run_id(step)
        )

    for step in (2, 1, 3):
        part_copy(step).start()
    summed = part[zl]
    for step in (1, 2, 3):
        part_copy(step).wait_recv()
    for step in (1, 2, 3):
        summed = summed + part_recv[step].astype(f32)
    out[0] = summed.astype(bf16)

    def drain(d, carry):
        for dz in range(4):
            id_plane(dz, d).wait_send()
            kv_copy(dz, d).wait_send()
        return carry

    lax.fori_loop(1, 16, drain, 0)
    for step in (1, 2, 3):
        id_z(step).wait_send()
        pos_z(step).wait_send()
        hid_run(step).wait_send()
        q_z(step).wait_send()
        o_copy(step).wait_send()
        st_copy(step).wait_send()
        part_copy(step).wait_send()
    for step in range(4):
        hid_pair(step).wait_send()
    wo_pair.wait_send()
    att_pair.wait_send()


def local(hidden, w_query, w_key, w_value, w_out, cache_keys, cache_values, stretch_count, stretch_ids, recompute_pos):
    half = np.arange(128) % 32
    freq = (ROPE_BASE ** (-(half * 2.0 / HEAD_DIM))).astype(np.float32)[None]
    vmem, smem, anywhere = (
        pl.BlockSpec(memory_space=pltpu.VMEM),
        pl.BlockSpec(memory_space=pltpu.SMEM),
        pl.BlockSpec(memory_space=pl.ANY),
    )
    f32, bf16, i32, dma = jnp.float32, jnp.bfloat16, jnp.int32, pltpu.SemaphoreType.DMA
    scratch = [
        pltpu.VMEM((8, 16, 2048), bf16),
        pltpu.VMEM((2048, 384), bf16),
        pltpu.VMEM((2, 128, 2048), bf16),
        pltpu.VMEM((256, 8, 128), f32),
        pltpu.VMEM((64, 1, 128), i32),
        pltpu.SMEM((64, 1, 128), i32),
        pltpu.VMEM((4, 1, 128), i32),
        pltpu.VMEM((4, 16, 96, 128), bf16),
        pltpu.VMEM((4, 16, 96, 128), bf16),
        pltpu.VMEM((4, 128, 128), bf16),
        pltpu.VMEM((2, 128, 128), bf16),
        pltpu.VMEM((48, 128), f32),
        pltpu.VMEM((48, 128), f32),
        pltpu.VMEM((16, 48, 128), i32),
        pltpu.VMEM((4, 128, 128), bf16),
        pltpu.VMEM((4, 128, 128), bf16),
        pltpu.VMEM((4, 4, 128), f32),
        pltpu.VMEM((4, 4, 128), f32),
        pltpu.VMEM((2, 4, 16, 128), bf16),
        pltpu.VMEM((4, 16, 128), bf16),
        pltpu.VMEM((4, 16, 2048), f32),
        pltpu.VMEM((4, 16, 2048), bf16),
        pltpu.VMEM((4, 16, 2048), bf16),
        dma((4,)),
        dma((4,)),
        dma((4,)),
        dma((4, 16)),
        dma((4, 16)),
        dma((4,)),
        dma((4,)),
        dma((4,)),
        dma((4,)),
        dma((4,)),
        dma((4, 16)),
        dma((4, 16)),
        dma((4,)),
        dma((4,)),
        dma((4,)),
        dma((4,)),
        dma((4,)),
        dma((4,)),
        dma((4,)),
        dma((4,)),
        dma,
        dma,
        dma,
        dma,
        dma((4,)),
        dma((4,)),
    ]
    return pl.pallas_call(
        kernel,
        out_shape=jax.ShapeDtypeStruct(hidden.shape, bf16),
        in_specs=[vmem, vmem, smem, vmem, vmem, vmem, vmem] + [anywhere] * 4,
        out_specs=vmem,
        scratch_shapes=scratch,
        compiler_params=pltpu.CompilerParams(
            collective_id=0, has_side_effects=True, vmem_limit_bytes=56 * 1024 * 1024
        ),
    )(
        hidden,
        stretch_ids,
        stretch_count,
        recompute_pos,
        jnp.asarray(freq),
        cache_keys,
        cache_values,
        w_query,
        w_key,
        w_value,
        w_out,
    )


def solution(mesh):
    placed = (
        P("group", "tp", None),
        P(None, "tp"),
        P(None, "tp"),
        P(None, "tp"),
        P("tp", None),
        P(None, "group", "tp"),
        P(None, "group", "tp"),
        P("group"),
        P("group", None),
        P("group", None),
    )
    return jax.shard_map(
        local, mesh=mesh, in_specs=placed, out_specs=P("group", "tp", None), check_vma=False
    )
```

time: 541 us -> 67.2 us (0.12)
  blocking collectives: 281 us -> 0 us
  waiting for transfers between devices: 74 us -> 0 us
  Pallas kernels: 0 us -> 64.9 us
  local copies, waits for them, and re-layouts: 63.8 us -> 1.47 us
  loops' own time: 36.4 us -> 0 us
  other arithmetic: 32.8 us -> 0 us
  matrix products: 21.4 us -> 0 us
  between operations: 14.4 us -> 0.66 us
  starting transfers between devices: 13.4 us -> 0 us
    all_gather x2 -> x0, blocking collectives: 250 us -> none  [the longest x1 200 us: local(): lax.all_gather(stretch_ids, 'group', axis=0, tiled=True)]
    reduce_scatter x1 -> x0, waiting for transfers between devices: 73.9 us -> none  [local(): lax.psum_scatter(jnp.dot(attention, w_out, preferred_element_type=jnp.flo...]
    pallas_call x0 -> x1, Pallas kernels: none -> 64.9 us  [local(): pl.pallas_call(kernel, out_shape=jax.ShapeDtypeStruct(hidden.shape, bf16)...]
    another operation x2 -> x0, loops' own time: 36.4 us -> none  [the longest x1 29.6 us: local(): lax.fori_loop(0, my_live, max_step, (start_max, lowest, empty_store))]
    unnamed x1 -> x0, blocking collectives: 30.7 us -> none
    dynamic_slice x46 -> x0, local copies, waits for them, and re-layouts: 26.6 us -> none  [the longest x18 9.93 us: sum_step(): scores = score_store[slot_index]]
    dot_general x23 -> x0, matrix products: 21.4 us -> none  [the longest x9 9.86 us: masked_scores(): jnp.einsum('qhd,khd->hqk', queries, key_buffer[slot_index], preferred_ele...]
    select_n x29 -> x0, other arithmetic: 15.8 us -> none  [the longest x9 5.76 us: max_step(): jnp.where(own_slot, their_max, jnp.maximum(their_max, slot_max))]
  transfers between devices with their start and end apart: 3 -> 0, of which waited for: 1 -> 0; matrix products, arithmetic and copies ran while one was open for 13% -> 0% of each run, Pallas kernels for 0% -> 0%
where the time goes in v1:
time: 67.2 us; the launch traced here: 67.1 us
  Pallas kernels  64.9 us (97%)
  local copies, waits for them, and re-layouts  1.47 us (2%)
    pallas_call x1, Pallas kernels, local(): pl.pallas_call(kernel, out_shape=jax.ShapeDtypeStruct(hidden.shape, bf16)...  64.9 us
    unnamed x1, local copies, waits for them, and re-layouts  1.47 us

profile of v1, /device:TPU:1, one launch (start us, length us, event | category | flops | bytes accessed | tf_op | source)
XLA Modules:
  0.0 67.1 jit_solution(8184745957346544987)
XLA Ops:
  0.7 64.9 %shard_map.109 = bf16[1,16,2048]{2,1,0:T(8,128)(2,1)} custom-call(bf16[1,16,2048]{2,1,0:T(8,128)(2,1)} %hidden.1, s32[1,12]{1,0:T(1,128)} %ids.1, s32[1]{0:T(128)S(6)} %copy.13.count, s32[1,128]{1,0:T(1,128)} %pos.1, f32[1,128]{1,0:T(1,128)} %constant.2.clone.freq, bf16[256,4,128]{2,1,0:T(4,128)(2,1)} %cache_keys.1, bf16[256,4,128]{2,1,0:T(4,128)(2,1)} %cache_values.1, ...), custom_call_target="tpu_custom_call" | custom-call | tf_op jit(solution)/shard_map/pallas_call | solution.py:482
  65.6 1.5 %copy.14 = bf16[1,16,2048]{2,1,0:T(8,128)(2,1)} copy(bf16[1,16,2048]{2,1,0:T(8,128)(2,1)} %shard_map.109) | data formatting | bytes 131072

commit v2 on v1

--- a/solution.py
+++ b/solution.py
@@ -17,6 +17,14 @@
 MASKED = -1e30
 FLOOR = -1e29
 FAR = 1 << 20
+OFFSETS = (
+    (0, 1), (0, 3), (1, 0), (3, 0),
+    (1, 1), (1, 3), (3, 1), (3, 3), (0, 2), (2, 0),
+    (1, 2), (2, 1), (3, 2), (2, 3), (2, 2),
+)
+STEP_X = sum(dx << (2 * i) for i, (dx, _) in enumerate(OFFSETS))
+STEP_Y = sum(dy << (2 * i) for i, (_, dy) in enumerate(OFFSETS))
+RINGS = ((0, 5), (5, 11), (11, 16))
 
 
 def kernel(
@@ -89,6 +97,14 @@
     zl, core = t // 2, t % 2
     other = 1 - core
 
+    def ahead(k):
+        shift = 2 * (k - 1)
+        return ((gx + (STEP_X >> shift) % 4) % 4) * 4 + (gy + (STEP_Y >> shift) % 4) % 4
+
+    def behind(k):
+        shift = 2 * (k - 1)
+        return ((gx + 4 - (STEP_X >> shift) % 4) % 4) * 4 + (gy + 4 - (STEP_Y >> shift) % 4) % 4
+
     def plane_id(idx):
         return (((idx // 4) * 4 + gz) * 4 + idx % 4, t)
 
@@ -119,11 +135,11 @@
     def greet(device):
         pl.semaphore_signal(barrier, inc=1, device_id=device, device_id_type=MESH)
 
-    for step in (2, 1, 3):
+    for step in (1, 3):
         greet(z_id(step))
 
-    def greet_plane(d, carry):
-        greet(plane_id((s + d) % 16))
+    def greet_plane(k, carry):
+        greet(plane_id(ahead(k)))
         return carry
 
     lax.fori_loop(1, 16, greet_plane, 0)
@@ -132,8 +148,8 @@
     greet(partner_id)
 
     lane = lax.broadcasted_iota(jnp.int32, (1, 128), 1)
-    ids_v[s] = jnp.where(lane == MAXCH, count[0], 0)
-    ids_v[s, :, 0:MAXCH] = ids[...]
+    ids_v[0] = jnp.where(lane == MAXCH, count[0], 0)
+    ids_v[0, :, 0:MAXCH] = ids[...]
     posz[0] = pos[...]
     rows = hidden[0].astype(f32)
     normed[t] = (rows * lax.rsqrt(jnp.mean(rows * rows, axis=-1, keepdims=True) + EPSILON)).astype(bf16)
@@ -154,37 +170,41 @@
     place = lax.broadcasted_iota(jnp.int32, (16, 48, 128), 0)
     key_pos[...] = (row48 // 4) * STRETCH + 4 * (16 * (place // 4) + 4 * gz + place % 4) + row48 % 4
 
-    pl.semaphore_wait(barrier, 22)
+    pl.semaphore_wait(barrier, 21)
 
     def id_z(step):
-        return remote(ids_v.at[s], ids_v.at[(4 - step) * 16 + s], sem_idz_s.at[step], sem_idz_r.at[4 - step], z_id(step))
-
-    def id_z_wait(dz):
-        here = ids_v.at[dz * 16 + s]
-        remote(here, here, sem_idz_s.at[dz], sem_idz_r.at[dz], z_id(1)).wait_recv()
+        return remote(ids_v.at[0], ids_v.at[(4 - step) * 16], sem_idz_s.at[step], sem_idz_r.at[4 - step], z_id(step))
 
     def pos_z(step):
         return remote(posz.at[0], posz.at[4 - step], sem_pos_s.at[step], sem_pos_r.at[4 - step], z_id(step))
 
-    def id_plane(dz, d):
-        here = ids_v.at[dz * 16 + s]
-        return remote(here, here, sem_idp_s.at[dz, d], sem_idp_r.at[dz, d], plane_id((s + d) % 16))
-
-    def id_plane_wait(dz, d):
-        here = ids_v.at[dz * 16 + (s + 16 - d) % 16]
-        return remote(here, here, sem_idp_s.at[dz, d], sem_idp_r.at[dz, d], plane_id((s + d) % 16))
+    id_relay = remote(ids_v.at[16], ids_v.at[32], sem_idz_s.at[2], sem_idz_r.at[2], z_id(3))
+    pos_relay = remote(posz.at[1], posz.at[2], sem_pos_s.at[2], sem_pos_r.at[2], z_id(3))
+
+    def wait_z(ref, send, recv, dz):
+        here = ref.at[dz]
+        remote(here, here, send.at[dz], recv.at[dz], z_id(1)).wait_recv()
+
+    def id_z_wait(dz):
+        here = ids_v.at[dz * 16]
+        remote(here, here, sem_idz_s.at[dz], sem_idz_r.at[dz], z_id(1)).wait_recv()
+
+    def id_plane(dz, k):
+        return remote(
+            ids_v.at[dz * 16], ids_v.at[dz * 16 + k], sem_idp_s.at[dz, k], sem_idp_r.at[dz, k], plane_id(ahead(k))
+        )
 
     def spread_ids(dz):
-        def body(d, carry):
-            id_plane(dz, d).start()
+        def body(k, carry):
+            id_plane(dz, k).start()
             return carry
 
         lax.fori_loop(1, 16, body, 0)
 
-    for step in (2, 1, 3):
+    for step in (1, 3):
         id_z(step).start()
     spread_ids(0)
-    for step in (2, 1, 3):
+    for step in (1, 3):
         pos_z(step).start()
 
     def hid_run(step):
@@ -203,7 +223,7 @@
         here = normed.at[((zl + 4 - step) % 4) * 2 + other]
         remote(here, here, sem_hidp_s.at[step], sem_hidp_r.at[step], partner_id).wait_recv()
 
-    for step in (1, 2, 3):
+    for step in (2, 1, 3):
         hid_run(step).start()
     hid_pair(0).start()
     loads[3].wait()
@@ -223,43 +243,53 @@
             target[quad * 16 : quad * 16 + 16, :] = jnp.concatenate(key_rows, 0).astype(bf16)
             target[48 + quad * 16 : 64 + quad * 16, :] = jnp.concatenate(value_rows, 0).astype(bf16)
 
-    def kv_copy(dz, d):
+    def kv_copy(dz, k):
         return remote(
-            kv_send.at[dz, d], kv.at[dz, s], sem_kv_s.at[dz, d], sem_kv_r.at[dz, d], plane_id((s + d) % 16)
+            kv_send.at[dz, k], kv.at[dz, s], sem_kv_s.at[dz, k], sem_kv_r.at[dz, k], plane_id(behind(k))
         )
 
-    def serve(dz):
-        def got(d, carry):
-            id_plane_wait(dz, d).wait_recv()
+    def serve(dz, ring, backward=False):
+        start, stop = ring
+
+        def got(k, carry):
+            id_plane(dz, k).wait_recv()
             return carry
 
-        lax.fori_loop(1, 16, got, 0)
-        here = pl.ds(dz * 16, 16)
-        to_smem = pltpu.make_async_copy(ids_v.at[here], ids_s.at[here], sem_smem.at[dz])
+        lax.fori_loop(max(start, 1), stop, got, 0)
+        here = pl.ds(dz * 16 + start, stop - start)
+        to_smem = pltpu.make_async_copy(ids_v.at[here], ids_s.at[here], sem_smem.at[dz, start])
         to_smem.start()
         to_smem.wait()
 
-        def send(d, carry):
-            fill(dz * 16 + (s + d) % 16, kv_send.at[dz, d])
-            kv_copy(dz, d).start()
+        def send(i, carry):
+            k = stop - 1 - i if backward else max(start, 1) + i
+            fill(dz * 16 + k, kv_send.at[dz, k])
+            kv_copy(dz, k).start()
             return carry
 
-        lax.fori_loop(1, 16, send, 0)
-        fill(dz * 16 + s, kv.at[dz, s])
-
+        lax.fori_loop(0, stop - max(start, 1), send, 0)
+        if start == 0:
+            fill(dz * 16, kv.at[dz, s])
+
+    serve(0, RINGS[0])
+    serve(0, RINGS[1])
     id_z_wait(1)
+    id_relay.start()
     spread_ids(1)
     id_z_wait(3)
     spread_ids(3)
-    serve(0)
-    id_z_wait(2)
-    spread_ids(2)
-    serve(1)
-    serve(3)
-
+    serve(0, RINGS[2])
+    serve(1, RINGS[0])
     for step in (1, 2, 3):
         hid_run_wait(step)
         hid_pair(step).start()
+    wait_z(posz, sem_pos_s, sem_pos_r, 1)
+    pos_relay.start()
+    serve(1, RINGS[1])
+    id_z_wait(2)
+    spread_ids(2)
+    serve(1, RINGS[2])
+
     posf = jnp.broadcast_to(pos[...].astype(f32), (128, 128)).T
     angle = posf * freq[...]
     cos_q, sin_q = jnp.cos(angle), jnp.sin(angle)
@@ -269,22 +299,27 @@
         load.wait()
     for step in range(4):
         hid_pair_wait(step)
-    projected = jnp.dot(normed[...].reshape(128, 2048), wqkv[...], preferred_element_type=f32)
+
+    def project(first, last):
+        return jnp.dot(normed[...].reshape(128, 2048), wqkv[:, first:last], preferred_element_type=f32)
 
     def rotate(values):
         swapped = jnp.where(lower, -pltpu.roll(values, 96, 1), pltpu.roll(values, 32, 1))
         return (values * cos_q + swapped * sin_q).astype(bf16)
 
-    qx[0] = (rotate(projected[:, 0:128]).astype(f32) * HEAD_DIM**-0.5).astype(bf16)
-    fresh[0] = rotate(projected[:, 128:256])
-    fresh[1] = projected[:, 256:384].astype(bf16)
+    qx[0] = (rotate(project(0, 128)).astype(f32) * HEAD_DIM**-0.5).astype(bf16)
 
     def q_z(step):
         return remote(qx.at[0], qx.at[4 - step], sem_q_s.at[step], sem_q_r.at[4 - step], z_id(step))
 
     for step in (2, 1, 3):
         q_z(step).start()
-    serve(2)
+    for ring in RINGS:
+        serve(2, ring)
+    serve(3, (0, 16), backward=True)
+    projected = project(128, 384)
+    fresh[0] = rotate(projected[:, 0:128])
+    fresh[1] = projected[:, 128:256].astype(bf16)
 
     head0 = lanes < 64
     swap_row = lax.broadcasted_iota(jnp.int32, (128, 128), 0)
@@ -314,8 +349,8 @@
 
     def attend(dz):
         def got(d, carry):
-            here = kv.at[dz, (s + 16 - d) % 16]
-            remote(here, here, sem_kv_s.at[dz, d], sem_kv_r.at[dz, d], plane_id((s + d) % 16)).wait_recv()
+            here = kv.at[dz, ahead(d)]
+            remote(here, here, sem_kv_s.at[dz, d], sem_kv_r.at[dz, d], plane_id(behind(d))).wait_recv()
             return carry
 
         lax.fori_loop(1, 16, got, 0)
@@ -328,7 +363,7 @@
         pos_col = jnp.broadcast_to(pos_row, (768, 128))
         same = jnp.where(place_of == pos_col, 1.0, 0.0).astype(bf16)
         marked = jnp.dot(same, ones, preferred_element_type=f32) > 0.5
-        limit = ids_s[dz * 16 + s, 0, MAXCH] * STRETCH
+        limit = ids_s[dz * 16, 0, MAXCH] * STRETCH
         usable = jnp.where(marked | (place_of >= limit), FAR, place_of) <= pos_col
         return soften(keys, values, qx[dz], usable)
 
@@ -337,24 +372,21 @@
 
     def st_copy(dz):
         return remote(st_send.at[dz], st_recv.at[4 - dz], sem_st_s.at[dz], sem_st_r.at[4 - dz], z_id(dz))
-
-    def wait_z(ref, send, recv, dz):
-        here = ref.at[dz]
-        remote(here, here, send.at[dz], recv.at[dz], z_id(1)).wait_recv()
 
     partials = [
         soften(fresh[0], fresh[1], qx[0], posf <= pos[...].astype(f32)),
         attend(0),
     ]
-    for dz in (1, 3, 2):
-        wait_z(posz, sem_pos_s, sem_pos_r, dz)
+    for dz in (1, 2, 3):
+        if dz > 1:
+            wait_z(posz, sem_pos_s, sem_pos_r, dz)
         wait_z(qx, sem_q_s, sem_q_r, dz)
         mixed, tops, sums = attend(dz)
         o_send[dz] = mixed.astype(bf16)
         st_send[dz] = jnp.concatenate(tops + sums, 0)
         o_copy(dz).start()
         st_copy(dz).start()
-    for dz in (1, 3, 2):
+    for dz in (3, 2, 1):
         wait_z(o_recv, sem_o_s, sem_o_r, dz)
         wait_z(st_recv, sem_st_s, sem_st_r, dz)
         stats = st_recv[dz]
@@ -405,9 +437,12 @@
         return carry
 
     lax.fori_loop(1, 16, drain, 0)
-    for step in (1, 2, 3):
+    for step in (1, 3):
         id_z(step).wait_send()
         pos_z(step).wait_send()
+    id_relay.wait_send()
+    pos_relay.wait_send()
+    for step in (1, 2, 3):
         hid_run(step).wait_send()
         q_z(step).wait_send()
         o_copy(step).wait_send()
@@ -457,7 +492,7 @@
         dma((4,)),
         dma((4, 16)),
         dma((4, 16)),
-        dma((4,)),
+        dma((4, 16)),
         dma((4,)),
         dma((4,)),
         dma((4,)),

time: 67.2 us -> 67.1 us (level)
  no operation moved by 1% of the time
where the time goes in v2:
time: 67.1 us; the launch traced here: 66.9 us
  Pallas kernels  64.8 us (97%)
  local copies, waits for them, and re-layouts  1.47 us (2%)
    pallas_call x1, Pallas kernels, local(): pl.pallas_call(kernel, out_shape=jax.ShapeDtypeStruct(hidden.shape, bf16)...  64.8 us
    unnamed x1, local copies, waits for them, and re-layouts  1.47 us

profile of v2, /device:TPU:1, one launch (start us, length us, event | category | flops | bytes accessed | tf_op | source)
XLA Modules:
  0.0 66.9 jit_solution(8972325747944270636)
XLA Ops:
  0.7 64.8 %shard_map.109 = bf16[1,16,2048]{2,1,0:T(8,128)(2,1)} custom-call(bf16[1,16,2048]{2,1,0:T(8,128)(2,1)} %hidden.1, s32[1,12]{1,0:T(1,128)} %ids.1, s32[1]{0:T(128)S(6)} %copy.13.count, s32[1,128]{1,0:T(1,128)} %pos.1, f32[1,128]{1,0:T(1,128)} %constant.2.clone.freq, bf16[256,4,128]{2,1,0:T(4,128)(2,1)} %cache_keys.1, bf16[256,4,128]{2,1,0:T(4,128)(2,1)} %cache_values.1, ...), custom_call_target="tpu_custom_call" | custom-call | tf_op jit(solution)/shard_map/pallas_call | solution.py:517
  65.4 1.5 %copy.14 = bf16[1,16,2048]{2,1,0:T(8,128)(2,1)} copy(bf16[1,16,2048]{2,1,0:T(8,128)(2,1)} %shard_map.109) | data formatting | bytes 131072

commit v3 on v2

--- a/solution.py
+++ b/solution.py
@@ -28,23 +28,28 @@
 
 
 def kernel(
-    hidden,
-    ids,
-    count,
-    pos,
+    hidden_in,
+    ids_in,
+    count_in,
+    pos_in,
     freq,
-    cache_keys,
-    cache_values,
+    keys_in,
+    values_in,
     w_query,
     w_key,
     w_value,
     w_out,
     out,
+    hidden,
+    ids,
+    count,
+    pos,
+    cache_keys,
+    cache_values,
     normed,
     wqkv,
     wo,
     cache32,
-    ids_v,
     ids_s,
     posz,
     kv_send,
@@ -68,7 +73,6 @@
     sem_idz_r,
     sem_idp_s,
     sem_idp_r,
-    sem_smem,
     sem_hid_s,
     sem_hid_r,
     sem_hidp_s,
@@ -127,15 +131,20 @@
         pltpu.make_async_copy(w_value, wqkv.at[:, 256:384], sem_load.at[2]),
         pltpu.make_async_copy(w_out, wo.at[0], sem_load.at[3]),
     ]
-    for load in loads:
-        load.start()
-
+    small = [
+        pltpu.make_async_copy(ids_in, ids, sem_load.at[4]),
+        pltpu.make_async_copy(count_in, count, sem_load.at[5]),
+        pltpu.make_async_copy(pos_in, pos, sem_load.at[6]),
+        pltpu.make_async_copy(hidden_in.at[0], hidden, sem_load.at[7]),
+        pltpu.make_async_copy(keys_in, cache_keys, sem_load.at[8]),
+        pltpu.make_async_copy(values_in, cache_values, sem_load.at[9]),
+    ]
     barrier = pltpu.get_barrier_semaphore()
 
     def greet(device):
         pl.semaphore_signal(barrier, inc=1, device_id=device, device_id_type=MESH)
 
-    for step in (1, 3):
+    for step in (2, 1, 3):
         greet(z_id(step))
 
     def greet_plane(k, carry):
@@ -147,11 +156,16 @@
         greet(run_id(step))
     greet(partner_id)
 
-    lane = lax.broadcasted_iota(jnp.int32, (1, 128), 1)
-    ids_v[0] = jnp.where(lane == MAXCH, count[0], 0)
-    ids_v[0, :, 0:MAXCH] = ids[...]
+    for load in small + loads:
+        load.start()
+    for load in small[:3]:
+        load.wait()
+    for slot in range(MAXCH):
+        ids_s[0, 0, slot] = ids[0, slot]
+    ids_s[0, 0, MAXCH] = count[0]
     posz[0] = pos[...]
-    rows = hidden[0].astype(f32)
+    small[3].wait()
+    rows = hidden[...].astype(f32)
     normed[t] = (rows * lax.rsqrt(jnp.mean(rows * rows, axis=-1, keepdims=True) + EPSILON)).astype(bf16)
 
     def widen(i, carry):
@@ -160,6 +174,8 @@
         cache32[here, 4:8, :] = cache_values[here].astype(f32)
         return carry
 
+    small[4].wait()
+    small[5].wait()
     lax.fori_loop(0, 8, widen, 0)
 
     row48 = lax.broadcasted_iota(jnp.int32, (48, 128), 0)
@@ -170,28 +186,25 @@
     place = lax.broadcasted_iota(jnp.int32, (16, 48, 128), 0)
     key_pos[...] = (row48 // 4) * STRETCH + 4 * (16 * (place // 4) + 4 * gz + place % 4) + row48 % 4
 
-    pl.semaphore_wait(barrier, 21)
+    pl.semaphore_wait(barrier, 22)
 
     def id_z(step):
-        return remote(ids_v.at[0], ids_v.at[(4 - step) * 16], sem_idz_s.at[step], sem_idz_r.at[4 - step], z_id(step))
+        return remote(ids_s.at[0], ids_s.at[(4 - step) * 16], sem_idz_s.at[step], sem_idz_r.at[4 - step], z_id(step))
 
     def pos_z(step):
         return remote(posz.at[0], posz.at[4 - step], sem_pos_s.at[step], sem_pos_r.at[4 - step], z_id(step))
-
-    id_relay = remote(ids_v.at[16], ids_v.at[32], sem_idz_s.at[2], sem_idz_r.at[2], z_id(3))
-    pos_relay = remote(posz.at[1], posz.at[2], sem_pos_s.at[2], sem_pos_r.at[2], z_id(3))
 
     def wait_z(ref, send, recv, dz):
         here = ref.at[dz]
         remote(here, here, send.at[dz], recv.at[dz], z_id(1)).wait_recv()
 
     def id_z_wait(dz):
-        here = ids_v.at[dz * 16]
+        here = ids_s.at[dz * 16]
         remote(here, here, sem_idz_s.at[dz], sem_idz_r.at[dz], z_id(1)).wait_recv()
 
     def id_plane(dz, k):
         return remote(
-            ids_v.at[dz * 16], ids_v.at[dz * 16 + k], sem_idp_s.at[dz, k], sem_idp_r.at[dz, k], plane_id(ahead(k))
+            ids_s.at[dz * 16], ids_s.at[dz * 16 + k], sem_idp_s.at[dz, k], sem_idp_r.at[dz, k], plane_id(ahead(k))
         )
 
     def spread_ids(dz):
@@ -201,11 +214,9 @@
 
         lax.fori_loop(1, 16, body, 0)
 
-    for step in (1, 3):
+    for step in (2, 1, 3):
         id_z(step).start()
     spread_ids(0)
-    for step in (1, 3):
-        pos_z(step).start()
 
     def hid_run(step):
         here = normed.at[t]
@@ -226,6 +237,8 @@
     for step in (2, 1, 3):
         hid_run(step).start()
     hid_pair(0).start()
+    for step in (2, 1, 3):
+        pos_z(step).start()
     loads[3].wait()
     wo_pair = remote(wo.at[0], wo.at[1], sem_wo_s, sem_wo_r, partner_id)
     wo_pair.start()
@@ -256,10 +269,6 @@
             return carry
 
         lax.fori_loop(max(start, 1), stop, got, 0)
-        here = pl.ds(dz * 16 + start, stop - start)
-        to_smem = pltpu.make_async_copy(ids_v.at[here], ids_s.at[here], sem_smem.at[dz, start])
-        to_smem.start()
-        to_smem.wait()
 
         def send(i, carry):
             k = stop - 1 - i if backward else max(start, 1) + i
@@ -274,20 +283,18 @@
     serve(0, RINGS[0])
     serve(0, RINGS[1])
     id_z_wait(1)
-    id_relay.start()
     spread_ids(1)
     id_z_wait(3)
     spread_ids(3)
     serve(0, RINGS[2])
     serve(1, RINGS[0])
+    serve(3, RINGS[0])
     for step in (1, 2, 3):
         hid_run_wait(step)
         hid_pair(step).start()
-    wait_z(posz, sem_pos_s, sem_pos_r, 1)
-    pos_relay.start()
-    serve(1, RINGS[1])
     id_z_wait(2)
     spread_ids(2)
+    serve(1, RINGS[1])
     serve(1, RINGS[2])
 
     posf = jnp.broadcast_to(pos[...].astype(f32), (128, 128)).T
@@ -314,9 +321,8 @@
 
     for step in (2, 1, 3):
         q_z(step).start()
-    for ring in RINGS:
-        serve(2, ring)
-    serve(3, (0, 16), backward=True)
+    serve(2, (0, 16), backward=True)
+    serve(3, (5, 16), backward=True)
     projected = project(128, 384)
     fresh[0] = rotate(projected[:, 0:128])
     fresh[1] = projected[:, 128:256].astype(bf16)
@@ -378,8 +384,7 @@
         attend(0),
     ]
     for dz in (1, 2, 3):
-        if dz > 1:
-            wait_z(posz, sem_pos_s, sem_pos_r, dz)
+        wait_z(posz, sem_pos_s, sem_pos_r, dz)
         wait_z(qx, sem_q_s, sem_q_r, dz)
         mixed, tops, sums = attend(dz)
         o_send[dz] = mixed.astype(bf16)
@@ -437,12 +442,9 @@
         return carry
 
     lax.fori_loop(1, 16, drain, 0)
-    for step in (1, 3):
+    for step in (1, 2, 3):
         id_z(step).wait_send()
         pos_z(step).wait_send()
-    id_relay.wait_send()
-    pos_relay.wait_send()
-    for step in (1, 2, 3):
         hid_run(step).wait_send()
         q_z(step).wait_send()
         o_copy(step).wait_send()
@@ -457,18 +459,19 @@
 def local(hidden, w_query, w_key, w_value, w_out, cache_keys, cache_values, stretch_count, stretch_ids, recompute_pos):
     half = np.arange(128) % 32
     freq = (ROPE_BASE ** (-(half * 2.0 / HEAD_DIM))).astype(np.float32)[None]
-    vmem, smem, anywhere = (
-        pl.BlockSpec(memory_space=pltpu.VMEM),
-        pl.BlockSpec(memory_space=pltpu.SMEM),
-        pl.BlockSpec(memory_space=pl.ANY),
-    )
+    vmem, anywhere = pl.BlockSpec(memory_space=pltpu.VMEM), pl.BlockSpec(memory_space=pl.ANY)
     f32, bf16, i32, dma = jnp.float32, jnp.bfloat16, jnp.int32, pltpu.SemaphoreType.DMA
     scratch = [
+        pltpu.VMEM(hidden.shape[1:], bf16),
+        pltpu.SMEM(stretch_ids.shape, i32),
+        pltpu.SMEM(stretch_count.shape, i32),
+        pltpu.VMEM(recompute_pos.shape, i32),
+        pltpu.VMEM(cache_keys.shape, bf16),
+        pltpu.VMEM(cache_values.shape, bf16),
         pltpu.VMEM((8, 16, 2048), bf16),
         pltpu.VMEM((2048, 384), bf16),
         pltpu.VMEM((2, 128, 2048), bf16),
         pltpu.VMEM((256, 8, 128), f32),
-        pltpu.VMEM((64, 1, 128), i32),
         pltpu.SMEM((64, 1, 128), i32),
         pltpu.VMEM((4, 1, 128), i32),
         pltpu.VMEM((4, 16, 96, 128), bf16),
@@ -487,10 +490,9 @@
         pltpu.VMEM((4, 16, 2048), f32),
         pltpu.VMEM((4, 16, 2048), bf16),
         pltpu.VMEM((4, 16, 2048), bf16),
-        dma((4,)),
-        dma((4,)),
-        dma((4,)),
-        dma((4, 16)),
+        dma((10,)),
+        dma((4,)),
+        dma((4,)),
         dma((4, 16)),
         dma((4, 16)),
         dma((4,)),
@@ -517,7 +519,7 @@
     return pl.pallas_call(
         kernel,
         out_shape=jax.ShapeDtypeStruct(hidden.shape, bf16),
-        in_specs=[vmem, vmem, smem, vmem, vmem, vmem, vmem] + [anywhere] * 4,
+        in_specs=[anywhere] * 4 + [vmem] + [anywhere] * 6,
         out_specs=vmem,
         scratch_shapes=scratch,
         compiler_params=pltpu.CompilerParams(

time: 67.1 us -> 64.1 us (0.955)
  Pallas kernels: 64.8 us -> 61.8 us
    pallas_call x1, Pallas kernels: 64.8 us -> 61.8 us  [local(): pl.pallas_call(kernel, out_shape=jax.ShapeDtypeStruct(hidden.shape, bf16)...]
where the time goes in v3:
time: 64.1 us; the launch traced here: 63.9 us
  Pallas kernels  61.8 us (96%)
  local copies, waits for them, and re-layouts  1.47 us (2%)
  between operations  0.66 us (1%)
    pallas_call x1, Pallas kernels, local(): pl.pallas_call(kernel, out_shape=jax.ShapeDtypeStruct(hidden.shape, bf16)...  61.8 us
    unnamed x1, local copies, waits for them, and re-layouts  1.47 us

profile of v3, /device:TPU:1, one launch (start us, length us, event | category | flops | bytes accessed | tf_op | source)
XLA Modules:
  0.0 63.9 jit_solution(17978650377751449195)
XLA Ops:
  0.7 61.8 %shard_map.109 = bf16[1,16,2048]{2,1,0:T(8,128)(2,1)} custom-call(bf16[1,16,2048]{2,1,0:T(8,128)(2,1)} %hidden_in.1, s32[1,12]{1,0:T(1,128)} %ids_in.1, s32[1]{0:T(128)S(6)} %copy.13.count_in, s32[1,128]{1,0:T(1,128)} %pos_in.1, f32[1,128]{1,0:T(1,128)} %constant.2.clone.freq, bf16[256,4,128]{2,1,0:T(4,128)(2,1)} %keys_in.1, bf16[256,4,128]{2,1,0:T(4,128)(2,1)} %values_in.1, ...), custom_call_target="tpu_custom_call" | custom-call | tf_op jit(solution)/shard_map/pallas_call | solution.py:519
  62.4 1.5 %copy.14 = bf16[1,16,2048]{2,1,0:T(8,128)(2,1)} copy(bf16[1,16,2048]{2,1,0:T(8,128)(2,1)} %shard_map.109) | data formatting | bytes 131072

commit v4 on v3

--- a/solution.py
+++ b/solution.py
@@ -63,8 +63,7 @@
     o_recv,
     st_send,
     st_recv,
-    att,
-    att_recv,
+    share,
     part,
     part_send,
     part_recv,
@@ -89,8 +88,6 @@
     sem_st_r,
     sem_wo_s,
     sem_wo_r,
-    sem_att_s,
-    sem_att_r,
     sem_part_s,
     sem_part_r,
 ):
@@ -115,6 +112,9 @@
     def z_id(step):
         return ((gx * 4 + (gz + step) % 4) * 4 + gy, t)
 
+    def z_half_id(step, half):
+        return ((gx * 4 + (gz + step) % 4) * 4 + gy, zl * 2 + half)
+
     def run_id(step):
         return (g, ((zl + step) % 4) * 2 + core)
 
@@ -129,7 +129,7 @@
         pltpu.make_async_copy(w_query, wqkv.at[:, 0:128], sem_load.at[0]),
         pltpu.make_async_copy(w_key, wqkv.at[:, 128:256], sem_load.at[1]),
         pltpu.make_async_copy(w_value, wqkv.at[:, 256:384], sem_load.at[2]),
-        pltpu.make_async_copy(w_out, wo.at[0], sem_load.at[3]),
+        pltpu.make_async_copy(w_out, wo.at[core], sem_load.at[3]),
     ]
     small = [
         pltpu.make_async_copy(ids_in, ids, sem_load.at[4]),
@@ -144,7 +144,13 @@
     def greet(device):
         pl.semaphore_signal(barrier, inc=1, device_id=device, device_id_type=MESH)
 
-    for step in (2, 1, 3):
+    late = gz // 2
+
+    @pl.when(late == 0)
+    def _():
+        greet(z_id(2))
+
+    for step in (1, 3):
         greet(z_id(step))
 
     def greet_plane(k, carry):
@@ -186,7 +192,7 @@
     place = lax.broadcasted_iota(jnp.int32, (16, 48, 128), 0)
     key_pos[...] = (row48 // 4) * STRETCH + 4 * (16 * (place // 4) + 4 * gz + place % 4) + row48 % 4
 
-    pl.semaphore_wait(barrier, 22)
+    pl.semaphore_wait(barrier, 21 + late)
 
     def id_z(step):
         return remote(ids_s.at[0], ids_s.at[(4 - step) * 16], sem_idz_s.at[step], sem_idz_r.at[4 - step], z_id(step))
@@ -214,7 +220,15 @@
 
         lax.fori_loop(1, 16, body, 0)
 
-    for step in (2, 1, 3):
+    id_relay = remote(ids_s.at[48], ids_s.at[32], sem_idz_s.at[0], sem_idz_r.at[2], z_id(1))
+    pos_relay = remote(posz.at[3], posz.at[2], sem_pos_s.at[0], sem_pos_r.at[2], z_id(1))
+    passing = (gz == 1) | (gz == 2)
+
+    @pl.when(late == 1)
+    def _():
+        id_z(2).start()
+
+    for step in (1, 3):
         id_z(step).start()
     spread_ids(0)
 
@@ -237,10 +251,14 @@
     for step in (2, 1, 3):
         hid_run(step).start()
     hid_pair(0).start()
-    for step in (2, 1, 3):
+    @pl.when(late == 1)
+    def _():
+        pos_z(2).start()
+
+    for step in (1, 3):
         pos_z(step).start()
     loads[3].wait()
-    wo_pair = remote(wo.at[0], wo.at[1], sem_wo_s, sem_wo_r, partner_id)
+    wo_pair = remote(wo.at[core], wo.at[core], sem_wo_s, sem_wo_r, partner_id)
     wo_pair.start()
 
     low_rows = lax.broadcasted_iota(jnp.int32, (8, 128), 0) < 4
@@ -282,10 +300,21 @@
 
     serve(0, RINGS[0])
     serve(0, RINGS[1])
+    id_z_wait(3)
+
+    @pl.when(passing)
+    def _():
+        id_relay.start()
+
+    spread_ids(3)
     id_z_wait(1)
     spread_ids(1)
-    id_z_wait(3)
-    spread_ids(3)
+    wait_z(posz, sem_pos_s, sem_pos_r, 3)
+
+    @pl.when(passing)
+    def _():
+        pos_relay.start()
+
     serve(0, RINGS[2])
     serve(1, RINGS[0])
     serve(3, RINGS[0])
@@ -321,7 +350,8 @@
 
     for step in (2, 1, 3):
         q_z(step).start()
-    serve(2, (0, 16), backward=True)
+    serve(2, RINGS[0])
+    serve(2, (5, 16), backward=True)
     serve(3, (5, 16), backward=True)
     projected = project(128, 384)
     fresh[0] = rotate(projected[:, 0:128])
@@ -373,50 +403,82 @@
         usable = jnp.where(marked | (place_of >= limit), FAR, place_of) <= pos_col
         return soften(keys, values, qx[dz], usable)
 
-    def o_copy(dz):
-        return remote(o_send.at[dz], o_recv.at[4 - dz], sem_o_s.at[dz], sem_o_r.at[4 - dz], z_id(dz))
-
-    def st_copy(dz):
-        return remote(st_send.at[dz], st_recv.at[4 - dz], sem_st_s.at[dz], sem_st_r.at[4 - dz], z_id(dz))
-
-    partials = [
-        soften(fresh[0], fresh[1], qx[0], posf <= pos[...].astype(f32)),
-        attend(0),
-    ]
+    def o_copy(dz, half):
+        device = z_half_id(dz, half)
+        return remote(
+            o_send.at[dz, half], o_recv.at[(4 - dz) % 4, core], sem_o_s.at[dz, half], sem_o_r.at[(4 - dz) % 4, core], device
+        )
+
+    def st_copy(dz, half):
+        device = z_half_id(dz, half)
+        return remote(
+            st_send.at[dz], st_recv.at[(4 - dz) % 4, core], sem_st_s.at[dz, half], sem_st_r.at[(4 - dz) % 4, core], device
+        )
+
+    def back_wait(dz, half):
+        here = o_recv.at[dz, half]
+        remote(here, here, sem_o_s.at[dz, half], sem_o_r.at[dz, half], partner_id).wait_recv()
+        here = st_recv.at[dz, half]
+        remote(here, here, sem_st_s.at[dz, half], sem_st_r.at[dz, half], partner_id).wait_recv()
+
+    def give(dz, mixed, tops, sums):
+        turned = mixed.T.astype(bf16)
+        for run in range(4):
+            for half in range(2):
+                o_send[dz, half, run] = turned[run * 32 + half * 16 : run * 32 + half * 16 + 16]
+        st_send[dz] = jnp.concatenate(tops + sums, 0)
+        o_copy(dz, other).start()
+        st_copy(dz, other).start()
+        if dz > 0:
+            o_copy(dz, core).start()
+            st_copy(dz, core).start()
+
+    fresh_mixed, fresh_tops, fresh_sums = soften(fresh[0], fresh[1], qx[0], posf <= pos[...].astype(f32))
+    own_mixed, own_tops, own_sums = attend(0)
+    halves, tops, sums = [], [], []
+    for head in range(2):
+        top = jnp.maximum(fresh_tops[head], own_tops[head])
+        fresh_factor, own_factor = jnp.exp(fresh_tops[head] - top), jnp.exp(own_tops[head] - top)
+        here = slice(head * 64, head * 64 + 64)
+        halves.append(fresh_mixed[here] * fresh_factor + own_mixed[here] * own_factor)
+        tops.append(top)
+        sums.append(fresh_sums[head] * fresh_factor + own_sums[head] * own_factor)
+    give(0, jnp.concatenate(halves, 0), tops, sums)
+    o_recv[0, core] = o_send[0, core]
+    st_recv[0, core] = st_send[0]
     for dz in (1, 2, 3):
-        wait_z(posz, sem_pos_s, sem_pos_r, dz)
+        if dz < 3:
+            wait_z(posz, sem_pos_s, sem_pos_r, dz)
         wait_z(qx, sem_q_s, sem_q_r, dz)
-        mixed, tops, sums = attend(dz)
-        o_send[dz] = mixed.astype(bf16)
-        st_send[dz] = jnp.concatenate(tops + sums, 0)
-        o_copy(dz).start()
-        st_copy(dz).start()
+        give(dz, *attend(dz))
+
+    wo_pair.wait_recv()
+    back_wait(0, other)
     for dz in (3, 2, 1):
-        wait_z(o_recv, sem_o_s, sem_o_r, dz)
-        wait_z(st_recv, sem_st_s, sem_st_r, dz)
-        stats = st_recv[dz]
-        partials.append(
-            (o_recv[dz].astype(f32), [stats[0:1], stats[1:2]], [stats[2:3], stats[3:4]])
-        )
-    halves = []
-    for head in range(2):
-        top = functools.reduce(jnp.maximum, [tops[head] for _, tops, _ in partials])
-        total, weight = 0.0, 0.0
-        for mixed, tops, sums in partials:
-            factor = jnp.exp(tops[head] - top)
-            total = total + mixed[head * 64 : head * 64 + 64] * factor
-            weight = weight + sums[head] * factor
-        halves.append(total / weight)
-    attention = jnp.concatenate(halves, 0).T.astype(bf16)
+        for half in range(2):
+            back_wait(dz, half)
+    stats = [[st_recv[dz, half] for half in range(2)] for dz in range(4)]
+    tops = [jnp.concatenate([one[0:2] for one in pair], 0) for pair in stats]
+    sums = [jnp.concatenate([one[2:4] for one in pair], 0) for pair in stats]
+    top = functools.reduce(jnp.maximum, tops)
+    factors = [jnp.exp(one - top) for one in tops]
+    weight = functools.reduce(jnp.add, [factor * one for factor, one in zip(factors, sums)])
+    shares = jnp.concatenate([factor / weight for factor in factors] + [jnp.zeros((112, 128), f32)], 0).T
     for run in range(4):
         for half in range(2):
-            att[half, run] = attention[run * 32 + half * 16 : run * 32 + half * 16 + 16]
-
-    att_pair = remote(att.at[other], att_recv, sem_att_s, sem_att_r, partner_id)
-    att_pair.start()
-    wo_pair.wait_recv()
-    att_pair.wait_recv()
-    mine = jnp.concatenate([att[core].reshape(64, 128), att_recv[...].reshape(64, 128)], 1)
+            share[half, run] = shares[run * 32 + half * 16 : run * 32 + half * 16 + 16]
+    own_share = share[core].reshape(64, 128)
+    first_head = lax.broadcasted_iota(jnp.int32, (64, 128), 1) < 64
+    sides = []
+    for half in range(2):
+        total = 0.0
+        for dz in range(4):
+            column = dz * 4 + half * 2
+            factor = jnp.where(first_head, own_share[:, column : column + 1], own_share[:, column + 1 : column + 2])
+            total = total + o_recv[dz, half].reshape(64, 128).astype(f32) * factor
+        sides.append(total.astype(bf16))
+
+    mine = jnp.concatenate(sides, 1)
     product = jnp.dot(mine, wo[...].reshape(256, 2048), preferred_element_type=f32).reshape(4, 16, 2048)
     part[...] = product
     part_send[...] = product.astype(bf16)
@@ -442,18 +504,32 @@
         return carry
 
     lax.fori_loop(1, 16, drain, 0)
-    for step in (1, 2, 3):
+    for step in (1, 3):
         id_z(step).wait_send()
         pos_z(step).wait_send()
+
+    @pl.when(late == 1)
+    def _():
+        id_z(2).wait_send()
+        pos_z(2).wait_send()
+
+    @pl.when(passing)
+    def _():
+        id_relay.wait_send()
+        pos_relay.wait_send()
+
+    for step in (1, 2, 3):
         hid_run(step).wait_send()
         q_z(step).wait_send()
-        o_copy(step).wait_send()
-        st_copy(step).wait_send()
+        for half in range(2):
+            o_copy(step, half).wait_send()
+            st_copy(step, half).wait_send()
         part_copy(step).wait_send()
     for step in range(4):
         hid_pair(step).wait_send()
     wo_pair.wait_send()
-    att_pair.wait_send()
+    o_copy(0, other).wait_send()
+    st_copy(0, other).wait_send()
 
 
 def local(hidden, w_query, w_key, w_value, w_out, cache_keys, cache_values, stretch_count, stretch_ids, recompute_pos):
@@ -481,12 +557,11 @@
         pltpu.VMEM((48, 128), f32),
         pltpu.VMEM((48, 128), f32),
         pltpu.VMEM((16, 48, 128), i32),
-        pltpu.VMEM((4, 128, 128), bf16),
-        pltpu.VMEM((4, 128, 128), bf16),
+        pltpu.VMEM((4, 2, 4, 16, 128), bf16),
+        pltpu.VMEM((4, 2, 4, 16, 128), bf16),
         pltpu.VMEM((4, 4, 128), f32),
-        pltpu.VMEM((4, 4, 128), f32),
-        pltpu.VMEM((2, 4, 16, 128), bf16),
-        pltpu.VMEM((4, 16, 128), bf16),
+        pltpu.VMEM((4, 2, 4, 128), f32),
+        pltpu.VMEM((2, 4, 16, 128), f32),
         pltpu.VMEM((4, 16, 2048), f32),
         pltpu.VMEM((4, 16, 2048), bf16),
         pltpu.VMEM((4, 16, 2048), bf16),
@@ -505,12 +580,10 @@
         dma((4,)),
         dma((4,)),
         dma((4,)),
-        dma((4,)),
-        dma((4,)),
-        dma((4,)),
-        dma((4,)),
-        dma,
-        dma,
+        dma((4, 2)),
+        dma((4, 2)),
+        dma((4, 2)),
+        dma((4, 2)),
         dma,
         dma,
         dma((4,)),

time: 64.1 us -> 61.5 us (0.959)
  the two profiles are of different devices: /device:TPU:1 before, /device:TPU:6 now
where the time goes in v4:
time: 61.5 us; the launch traced here: 61.3 us
  Pallas kernels  59.2 us (96%)
  local copies, waits for them, and re-layouts  1.47 us (2%)
  between operations  0.66 us (1%)
    pallas_call x1, Pallas kernels, local(): pl.pallas_call(kernel, out_shape=jax.ShapeDtypeStruct(hidden.shape, bf16)...  59.2 us
    unnamed x1, local copies, waits for them, and re-layouts  1.47 us

profile of v4, /device:TPU:6, one launch (start us, length us, event | category | flops | bytes accessed | tf_op | source)
XLA Modules:
  0.0 61.3 jit_solution(15437681069759811771)
XLA Ops:
  0.7 59.2 %shard_map.109 = bf16[1,16,2048]{2,1,0:T(8,128)(2,1)} custom-call(bf16[1,16,2048]{2,1,0:T(8,128)(2,1)} %hidden_in.1, s32[1,12]{1,0:T(1,128)} %ids_in.1, s32[1]{0:T(128)S(6)} %copy.13.count_in, s32[1,128]{1,0:T(1,128)} %pos_in.1, f32[1,128]{1,0:T(1,128)} %constant.2.clone.freq, bf16[256,4,128]{2,1,0:T(4,128)(2,1)} %keys_in.1, bf16[256,4,128]{2,1,0:T(4,128)(2,1)} %values_in.1, ...), custom_call_target="tpu_custom_call" | custom-call | tf_op jit(solution)/shard_map/pallas_call | solution.py:592
  59.9 1.5 %copy.14 = bf16[1,16,2048]{2,1,0:T(8,128)(2,1)} copy(bf16[1,16,2048]{2,1,0:T(8,128)(2,1)} %shard_map.109) | data formatting | bytes 131072

commit v5 on v4

--- a/solution.py
+++ b/solution.py
@@ -59,6 +59,9 @@
     key_cos,
     key_sin,
     key_pos,
+    pos_down,
+    query_cos,
+    query_sin,
     o_send,
     o_recv,
     st_send,
@@ -192,6 +195,11 @@
     place = lax.broadcasted_iota(jnp.int32, (16, 48, 128), 0)
     key_pos[...] = (row48 // 4) * STRETCH + 4 * (16 * (place // 4) + 4 * gz + place % 4) + row48 % 4
 
+    pos_down[...] = jnp.broadcast_to(pos[...].astype(f32), (128, 128)).T
+    angle = pos_down[...] * freq[...]
+    query_cos[...] = jnp.cos(angle)
+    query_sin[...] = jnp.sin(angle)
+
     pl.semaphore_wait(barrier, 21 + late)
 
     def id_z(step):
@@ -257,9 +265,7 @@
 
     for step in (1, 3):
         pos_z(step).start()
-    loads[3].wait()
     wo_pair = remote(wo.at[core], wo.at[core], sem_wo_s, sem_wo_r, partner_id)
-    wo_pair.start()
 
     low_rows = lax.broadcasted_iota(jnp.int32, (8, 128), 0) < 4
 
@@ -317,7 +323,6 @@
 
     serve(0, RINGS[2])
     serve(1, RINGS[0])
-    serve(3, RINGS[0])
     for step in (1, 2, 3):
         hid_run_wait(step)
         hid_pair(step).start()
@@ -326,9 +331,6 @@
     serve(1, RINGS[1])
     serve(1, RINGS[2])
 
-    posf = jnp.broadcast_to(pos[...].astype(f32), (128, 128)).T
-    angle = posf * freq[...]
-    cos_q, sin_q = jnp.cos(angle), jnp.sin(angle)
     lanes = lax.broadcasted_iota(jnp.int32, (128, 128), 1)
     lower = lanes % 64 < 32
     for load in loads[:3]:
@@ -341,7 +343,7 @@
 
     def rotate(values):
         swapped = jnp.where(lower, -pltpu.roll(values, 96, 1), pltpu.roll(values, 32, 1))
-        return (values * cos_q + swapped * sin_q).astype(bf16)
+        return (values * query_cos[...] + swapped * query_sin[...]).astype(bf16)
 
     qx[0] = (rotate(project(0, 128)).astype(f32) * HEAD_DIM**-0.5).astype(bf16)
 
@@ -350,9 +352,11 @@
 
     for step in (2, 1, 3):
         q_z(step).start()
+    loads[3].wait()
+    wo_pair.start()
     serve(2, RINGS[0])
     serve(2, (5, 16), backward=True)
-    serve(3, (5, 16), backward=True)
+    serve(3, (0, 16), backward=True)
     projected = project(128, 384)
     fresh[0] = rotate(projected[:, 0:128])
     fresh[1] = projected[:, 128:256].astype(bf16)
@@ -383,7 +387,19 @@
         mixed = lax.dot_general(values, jnp.concatenate(weights, 1), first_dims, preferred_element_type=f32)
         return jnp.concatenate([mixed[0:64, 0:128], mixed[64:128, 128:256]], 0), tops, sums
 
+    def visible(dz):
+        place_of = key_pos[...].reshape(768, 128)
+        pos_col = jnp.broadcast_to(posz[dz], (768, 128))
+        same = jnp.where(place_of == pos_col, 1.0, 0.0).astype(bf16)
+        marked = jnp.dot(same, ones, preferred_element_type=f32) > 0.5
+        limit = ids_s[dz * 16, 0, MAXCH] * STRETCH
+        return jnp.where(marked | (place_of >= limit), FAR, place_of) <= pos_col
+
     def attend(dz):
+        usable = visible(dz)
+        if dz > 0:
+            wait_z(qx, sem_q_s, sem_q_r, dz)
+
         def got(d, carry):
             here = kv.at[dz, ahead(d)]
             remote(here, here, sem_kv_s.at[dz, d], sem_kv_r.at[dz, d], plane_id(behind(d))).wait_recv()
@@ -394,13 +410,6 @@
         turned = jnp.dot(raw.reshape(768, 128), swap, preferred_element_type=f32).reshape(16, 48, 128)
         keys = (raw.astype(f32) * key_cos[...][None] + turned * key_sin[...][None]).astype(bf16).reshape(768, 128)
         values = kv[dz, :, 48:96, :].reshape(768, 128)
-        place_of = key_pos[...].reshape(768, 128)
-        pos_row = posz[dz]
-        pos_col = jnp.broadcast_to(pos_row, (768, 128))
-        same = jnp.where(place_of == pos_col, 1.0, 0.0).astype(bf16)
-        marked = jnp.dot(same, ones, preferred_element_type=f32) > 0.5
-        limit = ids_s[dz * 16, 0, MAXCH] * STRETCH
-        usable = jnp.where(marked | (place_of >= limit), FAR, place_of) <= pos_col
         return soften(keys, values, qx[dz], usable)
 
     def o_copy(dz, half):
@@ -433,7 +442,7 @@
             o_copy(dz, core).start()
             st_copy(dz, core).start()
 
-    fresh_mixed, fresh_tops, fresh_sums = soften(fresh[0], fresh[1], qx[0], posf <= pos[...].astype(f32))
+    fresh_mixed, fresh_tops, fresh_sums = soften(fresh[0], fresh[1], qx[0], pos_down[...] <= pos[...].astype(f32))
     own_mixed, own_tops, own_sums = attend(0)
     halves, tops, sums = [], [], []
     for head in range(2):
@@ -449,7 +458,6 @@
     for dz in (1, 2, 3):
         if dz < 3:
             wait_z(posz, sem_pos_s, sem_pos_r, dz)
-        wait_z(qx, sem_q_s, sem_q_r, dz)
         give(dz, *attend(dz))
 
     wo_pair.wait_recv()
@@ -557,6 +565,9 @@
         pltpu.VMEM((48, 128), f32),
         pltpu.VMEM((48, 128), f32),
         pltpu.VMEM((16, 48, 128), i32),
+        pltpu.VMEM((128, 128), f32),
+        pltpu.VMEM((128, 128), f32),
+        pltpu.VMEM((128, 128), f32),
         pltpu.VMEM((4, 2, 4, 16, 128), bf16),
         pltpu.VMEM((4, 2, 4, 16, 128), bf16),
         pltpu.VMEM((4, 4, 128), f32),

time: 61.5 us -> 61.4 us (level)
  the two profiles are of different devices: /device:TPU:6 before, /device:TPU:71 now
where the time goes in v5:
time: 61.4 us; the launch traced here: 61.2 us
  Pallas kernels  59.1 us (96%)
  local copies, waits for them, and re-layouts  1.47 us (2%)
  between operations  0.66 us (1%)
    pallas_call x1, Pallas kernels, local(): pl.pallas_call(kernel, out_shape=jax.ShapeDtypeStruct(hidden.shape, bf16)...  59.1 us
    unnamed x1, local copies, waits for them, and re-layouts  1.47 us

profile of v5, /device:TPU:71, one launch (start us, length us, event | category | flops | bytes accessed | tf_op | source)
XLA Modules:
  0.0 61.2 jit_solution(749265825664270996)
XLA Ops:
  0.7 59.1 %shard_map.109 = bf16[1,16,2048]{2,1,0:T(8,128)(2,1)} custom-call(bf16[1,16,2048]{2,1,0:T(8,128)(2,1)} %hidden_in.1, s32[1,12]{1,0:T(1,128)} %ids_in.1, s32[1]{0:T(128)S(6)} %copy.13.count_in, s32[1,128]{1,0:T(1,128)} %pos_in.1, f32[1,128]{1,0:T(1,128)} %constant.2.clone.freq, bf16[256,4,128]{2,1,0:T(4,128)(2,1)} %keys_in.1, bf16[256,4,128]{2,1,0:T(4,128)(2,1)} %values_in.1, ...), custom_call_target="tpu_custom_call" | custom-call | tf_op jit(solution)/shard_map/pallas_call | solution.py:603
  59.7 1.5 %copy.14 = bf16[1,16,2048]{2,1,0:T(8,128)(2,1)} copy(bf16[1,16,2048]{2,1,0:T(8,128)(2,1)} %shard_map.109) | data formatting | bytes 131072

commit v6 on v5

--- a/solution.py
+++ b/solution.py
@@ -122,6 +122,7 @@
         return (g, ((zl + step) % 4) * 2 + core)
 
     partner_id = (g, zl * 2 + other)
+    crossing_first = (2, 3 - 2 * (zl % 2), 1 + 2 * (zl % 2))
 
     def remote(src, dst, send, recv, device):
         return pltpu.make_async_remote_copy(
@@ -256,7 +257,7 @@
         here = normed.at[((zl + 4 - step) % 4) * 2 + other]
         remote(here, here, sem_hidp_s.at[step], sem_hidp_r.at[step], partner_id).wait_recv()
 
-    for step in (2, 1, 3):
+    for step in crossing_first:
         hid_run(step).start()
     hid_pair(0).start()
     @pl.when(late == 1)
@@ -496,7 +497,7 @@
             part_send.at[(zl + step) % 4], part_recv.at[step], sem_part_s.at[step], sem_part_r.at[step], run_id(step)
         )
 
-    for step in (2, 1, 3):
+    for step in crossing_first:
         part_copy(step).start()
     summed = part[zl]
     for step in (1, 2, 3):

time: 61.4 us -> 61.4 us (level)
  the two profiles are of different devices: /device:TPU:71 before, /device:TPU:67 now
where the time goes in v6:
time: 61.4 us; the launch traced here: 61.2 us
  Pallas kernels  59.1 us (96%)
  local copies, waits for them, and re-layouts  1.47 us (2%)
  between operations  0.66 us (1%)
    pallas_call x1, Pallas kernels, local(): pl.pallas_call(kernel, out_shape=jax.ShapeDtypeStruct(hidden.shape, bf16)...  59.1 us
    unnamed x1, local copies, waits for them, and re-layouts  1.47 us

profile of v6, /device:TPU:67, one launch (start us, length us, event | category | flops | bytes accessed | tf_op | source)
XLA Modules:
  0.0 61.2 jit_solution(7231764977436724973)
XLA Ops:
  0.7 59.1 %shard_map.109 = bf16[1,16,2048]{2,1,0:T(8,128)(2,1)} custom-call(bf16[1,16,2048]{2,1,0:T(8,128)(2,1)} %hidden_in.1, s32[1,12]{1,0:T(1,128)} %ids_in.1, s32[1]{0:T(128)S(6)} %copy.13.count_in, s32[1,128]{1,0:T(1,128)} %pos_in.1, f32[1,128]{1,0:T(1,128)} %constant.2.clone.freq, bf16[256,4,128]{2,1,0:T(4,128)(2,1)} %keys_in.1, bf16[256,4,128]{2,1,0:T(4,128)(2,1)} %values_in.1, ...), custom_call_target="tpu_custom_call" | custom-call | tf_op jit(solution)/shard_map/pallas_call | solution.py:604
  59.8 1.5 %copy.14 = bf16[1,16,2048]{2,1,0:T(8,128)(2,1)} copy(bf16[1,16,2048]{2,1,0:T(8,128)(2,1)} %shard_map.109) | data formatting | bytes 131072
